TPU v7x, 512 devices: a whole 4x4x16 slice. The times are simulated.
512 devices in a mesh: seq: 128 (over x, y, z_lo, core), head: 4 (over z_hi).
Axes of the slice: x: 4, y: 4, z: 16 (z_hi: 4, z_lo: 4; z = z_hi * 4 + z_lo), core: 2. Of those that a mesh axis runs over, the one named last changes fastest.
Arguments:
- queries: bfloat16 [16, 32768, 128], P('head', 'seq'), may hold values from -9 to 9
- key_vectors: bfloat16 [16, 32768, 128], P('head', 'seq'), may hold values from -9 to 9
- value_vectors: bfloat16 [16, 32768, 128], P('head', 'seq'), may hold values from -16 to 16
- block_perm: int32 [16, 64], P('head'), may hold values from 0 to 63, each once within a row
- out_weight: bfloat16 [16, 128, 2048], P('head'), may hold values from -0.125 to 0.125
- out_cotangent: bfloat16 [32768, 2048], P('seq', 'head'), may hold values from -6 to 6
Outputs:
- projected: bfloat16 [32768, 2048], P('seq', 'head')
- gradient_of_queries: bfloat16 [16, 32768, 128], P('head', 'seq')
- key_grad: bfloat16 [16, 32768, 128], P('head', 'seq')
- value_grad: bfloat16 [16, 32768, 128], P('head', 'seq')
Inputs may be any that keep to these rules, and one draw needn't show every extreme that they name: Each row of block_perm names every block of 0 to 63 once.
All inputs are finite; a program needn't handle non-finite values.
Results may differ from a plain program's by a relative error of at most 0.029.
Values may be sent and summed in bfloat16 or wider, within the bound.
A program may use at most 64 MiB of HBM per device.

v0:
```python
import math
import jax
import jax.numpy as jnp
from jax import lax
from jax.sharding import PartitionSpec as P


def partner(shard, axis, bit):
    return lax.ppermute(shard, axis, [(i, i ^ 1 << bit) for i in range(lax.axis_size(axis))])


def per_device(queries, key_vectors, value_vectors, block_perm, out_weight, out_cotangent):
    devices = lax.axis_size("seq")
    position = lax.axis_index("seq")
    parity = position % 2
    group_heads, tok_rows, head_width = queries.shape
    portion = tok_rows * head_width // devices
    score_scale = 1.0 / math.sqrt(head_width)
    owners = jnp.repeat(block_perm, 2, axis=1)
    indices = lax.iota(jnp.int32, devices)
    sources = [2 * owners, 2 * owners + 1]
    source_table = jnp.stack(sources, axis=1)
    slot_count = source_table.shape[1]
    select = (source_table[..., None] == indices).astype(jnp.bfloat16)
    stacked = jnp.stack([key_vectors, value_vectors])
    spread = lax.all_to_all(
        stacked.reshape(2, group_heads, devices, portion),
        "seq",
        split_axis=2,
        concat_axis=2,
        tiled=True,
    )
    picked = jnp.einsum(
        "hsij,chjl->chsil", select, spread, preferred_element_type=jnp.float32
    ).astype(jnp.bfloat16)
    routed = lax.all_to_all(picked, "seq", split_axis=3, concat_axis=3, tiled=True)
    routed = routed.reshape(2, group_heads, slot_count, tok_rows, head_width)
    partner_kv = routed.reshape(2, group_heads, 2 * tok_rows, head_width)
    pair_other = partner(stacked, "seq", 0)
    local_kv = jnp.where(
        parity == 0,
        jnp.concatenate([stacked, pair_other], 2),
        jnp.concatenate([pair_other, stacked], 2),
    )
    combined = jnp.concatenate([local_kv, partner_kv], 2)
    key_all = combined[0]
    value_all = combined[1]
    logit_scores = (
        jnp.einsum("htd,hkd->htk", queries, key_all, preferred_element_type=jnp.float32)
        * score_scale
    )
    row_max = jnp.max(logit_scores, axis=-1, keepdims=True)
    weights = jnp.exp(logit_scores - row_max)
    probabilities = weights / jnp.sum(weights, axis=-1, keepdims=True)
    reduced_probabilities = probabilities.astype(jnp.bfloat16)
    attention_result = jnp.einsum(
        "htk,hkd->htd", reduced_probabilities, value_all, preferred_element_type=jnp.float32
    ).astype(jnp.bfloat16)
    partial_out = jnp.einsum(
        "htd,hde->te", attention_result, out_weight, preferred_element_type=jnp.float32
    )
    summed = lax.psum(partial_out.astype(jnp.bfloat16), "head").astype(jnp.float32)
    columns = summed.shape[1] // lax.axis_size("head")
    result = lax.dynamic_slice_in_dim(summed, lax.axis_index("head") * columns, columns, 1)
    projected = result.astype(jnp.bfloat16)
    full_grad = lax.all_gather(out_cotangent, "head", axis=1, tiled=True)
    grad_att = jnp.einsum(
        "te,hde->htd", full_grad, out_weight, preferred_element_type=jnp.float32
    ).astype(jnp.bfloat16)
    row_delta = jnp.sum(
        grad_att.astype(jnp.float32) * attention_result.astype(jnp.float32), axis=-1, keepdims=True
    )
    probability_gradient = jnp.einsum(
        "htd,hkd->htk", grad_att, value_all, preferred_element_type=jnp.float32
    )
    score_gradient = (probabilities * (probability_gradient - row_delta) * score_scale).astype(
        jnp.bfloat16
    )
    gradient_of_queries = jnp.einsum(
        "htk,hkd->htd", score_gradient, key_all, preferred_element_type=jnp.float32
    ).astype(jnp.bfloat16)
    key_part = jnp.einsum(
        "htk,htd->hkd", score_gradient, queries, preferred_element_type=jnp.float32
    )
    value_part = jnp.einsum(
        "htk,htd->hkd", reduced_probabilities, grad_att, preferred_element_type=jnp.float32
    )
    gradients = jnp.stack([key_part, value_part])
    block_rows = 2 * tok_rows
    local_grad = gradients[:, :, :block_rows].reshape(2, group_heads, 2, tok_rows, head_width)
    own_grad = jnp.where(parity == 0, local_grad[:, :, 0], local_grad[:, :, 1])
    other_grad = jnp.where(parity == 0, local_grad[:, :, 1], local_grad[:, :, 0]).astype(
        jnp.bfloat16
    )
    partner_grad = gradients[:, :, block_rows:].reshape(2, group_heads, 2, tok_rows, head_width)
    partner_grad = partner_grad.astype(jnp.bfloat16)
    returned = lax.all_to_all(
        partner_grad.reshape(2, group_heads, slot_count, devices, portion),
        "seq",
        split_axis=3,
        concat_axis=3,
        tiled=True,
    )
    summed_back = jnp.einsum(
        "hsij,chsil->chjl", select, returned, preferred_element_type=jnp.float32
    ).astype(jnp.bfloat16)
    arrived = lax.all_to_all(summed_back, "seq", split_axis=2, concat_axis=2, tiled=True)
    arrived = arrived.reshape(2, group_heads, tok_rows, head_width).astype(jnp.float32)
    pair_back = partner(other_grad, "seq", 0).astype(jnp.float32)
    total_grad = own_grad + arrived + pair_back
    key_grad = total_grad[0].astype(jnp.bfloat16)
    value_grad = total_grad[1].astype(jnp.bfloat16)
    return (projected, gradient_of_queries, key_grad, value_grad)


def solution(mesh):
    return jax.shard_map(
        per_device,
        mesh=mesh,
        in_specs=(
            P("head", "seq", None),
            P("head", "seq", None),
            P("head", "seq", None),
            P("head", None),
            P("head", None, None),
            P("seq", "head"),
        ),
        out_specs=(
            P("seq", "head"),
            P("head", "seq", None),
            P("head", "seq", None),
            P("head", "seq", None),
        ),
        check_vma=False,
    )
```

profile of v0, /device:TPU:2, one launch (start us, length us, event | category | flops | bytes accessed | tf_op | source)
XLA Modules:
  0.0 314.9 jit_solution(3298835082028819904)
XLA Ops:
  9.5 1.3 copy.72
  10.8 13.0 %all-to-all-start = ((bf16[2,4,128,256]{3,0,1,2:T(2,128)(2,1)}), bf16[2,4,128,256]{3,0,1,2:T(2,128)(2,1)S(1)}, u32[]{:S(2)}, u32[]{:S(2)}) async-start(bf16[2,4,128,256]{3,0,1,2:T(2,128)(2,1)} %copy.72), calls=%async_computation | async-start | bytes 1048576 | tf_op jit(solution)/shard_map/all_to_all | solution.py:26
  24.1 16.4 %all-to-all-done = bf16[2,4,128,256]{3,0,1,2:T(2,128)(2,1)S(1)} async-done(((bf16[2,4,128,256]{3,0,1,2:T(2,128)(2,1)}), bf16[2,4,128,256]{3,0,1,2:T(2,128)(2,1)S(1)}, u32[]{:S(2)}, u32[]{:S(2)}) %all-to-all-start) | async-done | bytes 524320 | tf_op jit(solution)/shard_map/all_to_all | solution.py:26
  41.2 1.7 fusion.11
  42.9 2.1 copy.76
  45.0 9.3 %all-to-all-start.1 = ((bf16[2,4,2,128,256]{4,2,0,1,3:T(2,128)(2,1)}), bf16[2,4,2,128,256]{4,2,0,1,3:T(2,128)(2,1)}, u32[]{:S(2)}, u32[]{:S(2)}) async-start(bf16[2,4,2,128,256]{4,2,0,1,3:T(2,128)(2,1)} %copy.76), calls=%async_computation.1 | async-start | bytes 2097152 | tf_op jit(solution)/shard_map/all_to_all | solution.py:36
  54.5 2.2 collective-permute-start
  56.7 1.7 collective-permute-done
  58.4 1.6 maximum_select_fusion
  60.1 21.5 %all-to-all-done.1 = bf16[2,4,2,128,256]{4,2,0,1,3:T(2,128)(2,1)} async-done(((bf16[2,4,2,128,256]{4,2,0,1,3:T(2,128)(2,1)}), bf16[2,4,2,128,256]{4,2,0,1,3:T(2,128)(2,1)}, u32[]{:S(2)}, u32[]{:S(2)}) %all-to-all-start.1) | async-done | bytes 1048608 | tf_op jit(solution)/shard_map/all_to_all | solution.py:36
  81.6 2.5 copy.77
  84.1 2.3 reshape_reshape.3
  86.4 2.1 fusion.15
  88.5 4.6 %fusion.36 = (f32[4,256]{1,0:T(4,128)S(1)}, f32[4,256,1024]{1,2,0:T(8,128)}) fusion(bf16[4,1024,128]{2,1,0:T(8,128)(2,1)} %fusion.15, bf16[4,256,128]{2,1,0:T(8,128)(2,1)S(1)} %copy-done.15), kind=kOutput, calls=%fused_computation.63 | convolution fusion | flops 271582208 | bytes 5509120 | tf_op jit(solution)/shard_map/sub | solution.py:53
  93.1 2.6 fusion.10
  95.7 1.3 copy-done.3
  97.6 16.3 %all-gather.2.cloned.1.call-done = bf16[256,2048]{1,0:T(8,128)(2,1)} async-done(((bf16[256,512]{1,0:T(8,128)(2,1)}), bf16[256,2048]{1,0:T(8,128)(2,1)}) %all-gather.2.cloned.1.call-update) | async-done | bytes 1048592 | tf_op jit(solution)/shard_map/all_gather | solution.py:66
  113.9 2.1 fusion.22
  119.8 1.3 copy-done.2
  121.3 1.3 convert_element_type.88
  122.5 2.3 copy.86
  124.8 45.1 %all_to_all.20 = bf16[2,4,2,128,256]{4,2,0,1,3:T(2,128)(2,1)S(1)} all-to-all(bf16[2,4,2,128,256]{4,2,0,1,3:T(2,128)(2,1)S(1)} %copy.86), channel_id=1, replica_groups=mesh['seq'=128,'head'=4] {'seq'}, dimensions={3} | all-to-all | bytes 2097152 | tf_op jit(solution)/shard_map/all_to_all | solution.py:97
  171.9 8.6 %all-to-all-start.3 = ((bf16[2,4,128,256]{3,0,1,2:T(2,128)(2,1)}), bf16[2,4,128,256]{3,0,1,2:T(2,128)(2,1)S(1)}, u32[]{:S(2)}, u32[]{:S(2)}) async-start(bf16[2,4,128,256]{3,0,1,2:T(2,128)(2,1)} %copy.88), calls=%async_computation.3 | async-start | bytes 1048576 | tf_op jit(solution)/shard_map/all_to_all | solution.py:107
  180.6 1.8 fusion.6
  182.4 1.8 fusion.7
  184.3 1.3 copy-done.5
  186.4 2.0 collective-permute-start.1
  188.5 1.6 convolution_convert_fusion.1
  190.1 111.2 %all-reduce.2.cloned.1.call-done = bf16[256,2048]{1,0:T(8,128)(2,1)} async-done(((bf16[256,2048]{1,0:T(8,128)(2,1)}), bf16[256,2048]{1,0:T(8,128)(2,1)}) %all-reduce.2.cloned.1.call-update) | async-done | bytes 1048592 | tf_op jit(solution)/shard_map/psum | solution.py:62
  301.3 1.7 convert_convert_fusion
  304.0 1.3 reshape.55
  305.3 1.9 fusion.18
  (59 shorter events, 12.7 us)
Async XLA Ops:
  7.2 106.8 %copy-start = (bf16[4,128,2048]{2,1,0:T(8,128)(2,1)S(1)}, bf16[4,128,2048]{2,1,0:T(8,128)(2,1)}, u32[]{:S(2)}) copy-start(bf16[4,128,2048]{2,1,0:T(8,128)(2,1)} %param.10) | copy-start | bytes 6291460
  7.2 16.6 %copy-start.17 = (s32[4,64]{1,0:T(4,128)S(1)}, s32[4,64]{1,0:T(4,128)}, u32[]{:S(2)}) copy-start(s32[4,64]{1,0:T(4,128)} %param.9) | copy-start | bytes 3076
  10.8 29.6 %all-to-all-start = ((bf16[2,4,128,256]{3,0,1,2:T(2,128)(2,1)}), bf16[2,4,128,256]{3,0,1,2:T(2,128)(2,1)S(1)}, u32[]{:S(2)}, u32[]{:S(2)}) async-start(bf16[2,4,128,256]{3,0,1,2:T(2,128)(2,1)} %copy.72), calls=%async_computation | async-start | bytes 1048576 | tf_op jit(solution)/shard_map/all_to_all | solution.py:26
  40.4 0.8 copy-start.14
  42.9 11.5 %copy-start.12 = (bf16[4,256,128]{2,1,0:T(8,128)(2,1)S(1)}, bf16[4,256,128]{2,1,0:T(8,128)(2,1)}, u32[]{:S(2)}) copy-start(bf16[4,256,128]{2,1,0:T(8,128)(2,1)} %param.8) | copy-start | bytes 786436
  45.0 9.4 %copy-start.13 = (bf16[4,256,128]{2,1,0:T(8,128)(2,1)S(1)}, bf16[4,256,128]{2,1,0:T(8,128)(2,1)}, u32[]{:S(2)}) copy-start(bf16[4,256,128]{2,1,0:T(8,128)(2,1)} %param.7) | copy-start | bytes 786436
  45.0 36.6 %all-to-all-start.1 = ((bf16[2,4,2,128,256]{4,2,0,1,3:T(2,128)(2,1)}), bf16[2,4,2,128,256]{4,2,0,1,3:T(2,128)(2,1)}, u32[]{:S(2)}, u32[]{:S(2)}) async-start(bf16[2,4,2,128,256]{4,2,0,1,3:T(2,128)(2,1)} %copy.76), calls=%async_computation.1 | async-start | bytes 2097152 | tf_op jit(solution)/shard_map/all_to_all | solution.py:36
  54.3 59.6 %all-gather.2.cloned.1.call-start = ((), (), s32[]{:S(2)}) async-start(), calls=%async_computation.5 | async-start | bytes 1310720 | tf_op jit(solution)/shard_map/all_gather | solution.py:66
  54.5 3.9 %collective-permute-start = (bf16[2,4,256,128]{3,2,1,0:T(8,128)(2,1)S(1)}, bf16[2,4,256,128]{3,2,1,0:T(8,128)(2,1)}, u32[]{:S(2)}, u32[]{:S(2)}) collective-permute-start(bf16[2,4,256,128]{3,2,1,0:T(8,128)(2,1)S(1)} %pad_maximum_fusion.2), channel_id=1, source_target_pairs={{0,4},{4,0},{8,12},{12,8},{16,20},{20,16},{24,28},{28,24},{32,36},... | collective-permute-start | bytes 1572872 | tf_op jit(solution)/shard_map/ppermute | solution.py:9
  86.4 2.1 copy-start.15
  93.1 4.0 %copy-start.6 = (bf16[2,4,512,128]{3,2,1,0:T(8,128)(2,1)S(1)}, bf16[2,4,512,128]{3,2,1,0:T(8,128)(2,1)}, u32[]{:S(2)}) copy-start(bf16[2,4,512,128]{3,2,1,0:T(8,128)(2,1)} %reshape_reshape.3) | copy-start | bytes 3145732
  95.7 1.3 copy-start.3
  113.9 2.1 copy-start.4
  113.9 3.1 copy-start.11
  116.1 1.5 copy-start.7
  116.8 2.4 copy-start.1
  117.5 0.9 copy-start.16
  118.5 1.3 copy-start.8
  119.8 1.3 copy-start.2
  171.9 131.0 %all-to-all-start.3 = ((bf16[2,4,128,256]{3,0,1,2:T(2,128)(2,1)}), bf16[2,4,128,256]{3,0,1,2:T(2,128)(2,1)S(1)}, u32[]{:S(2)}, u32[]{:S(2)}) async-start(bf16[2,4,128,256]{3,0,1,2:T(2,128)(2,1)} %copy.88), calls=%async_computation.3 | async-start | bytes 1048576 | tf_op jit(solution)/shard_map/all_to_all | solution.py:107
  180.5 120.8 %all-reduce.2.cloned.1.call-start = ((), (), s32[]{:S(2)}) async-start(), calls=%async_computation.4 | async-start | bytes 2097152 | tf_op jit(solution)/shard_map/psum | solution.py:62
  182.4 6.1 %copy-start.9 = (bf16[4,256,1024]{1,2,0:T(8,128)(2,1)S(1)}, bf16[4,256,1024]{1,2,0:T(8,128)(2,1)}, u32[]{:S(2)}) copy-start(bf16[4,256,1024]{1,2,0:T(8,128)(2,1)} %copy-done.8) | copy-start | bytes 6291460
  182.4 6.1 %copy-start.10 = (bf16[4,1024,128]{2,1,0:T(8,128)(2,1)S(1)}, bf16[4,1024,128]{2,1,0:T(8,128)(2,1)}, u32[]{:S(2)}) copy-start(bf16[4,1024,128]{2,1,0:T(8,128)(2,1)} %fusion.15) | copy-start | bytes 3145732
  184.2 1.3 copy-start.5
  186.4 118.9 %collective-permute-start.1 = (bf16[2,4,256,128]{3,2,1,0:T(8,128)(2,1)}, bf16[2,4,256,128]{3,2,1,0:T(8,128)(2,1)}, u32[]{:S(2)}, u32[]{:S(2)}) collective-permute-start(bf16[2,4,256,128]{3,2,1,0:T(8,128)(2,1)} %fusion.21), channel_id=1, source_target_pairs={{0,4},{4,0},{8,12},{12,8},{16,20},{20,16},{24,28},{28,24},{32,36},... | collective-permute-start | bytes 1572872 | tf_op jit(solution)/shard_map/ppermute | solution.py:9
Sparse Core Ops, SparseCore 0:
  57.3 56.6 all-gather.1
  184.3 116.9 all-reduce.1
where the time goes:
time: 316 us; the launch traced here: 315 us
  waiting for transfers between devices  167 us (53%)
  blocking collectives  45.1 us (14%)
  starting transfers between devices  35.3 us (11%)
  local copies, waits for them, and re-layouts  23.7 us (8%)
  matrix products  15.4 us (5%)
  between operations  14.4 us (5%)
  other arithmetic  14.1 us (4%)
    psum x1, waiting for transfers between devices, per_device(): lax.psum(partial_out.astype(jnp.bfloat16), 'head').astype(jnp.float32)  111 us
    all_to_all x1, blocking collectives, per_device(): lax.all_to_all(partner_grad.reshape(2, group_heads, slot_count, devices,...  45.1 us
    all_to_all x1, waiting for transfers between devices, per_device(): lax.all_to_all(picked, 'seq', split_axis=3, concat_axis=3, tiled=True)  21.5 us
    all_to_all x1, waiting for transfers between devices, per_device(): lax.all_to_all(stacked.reshape(2, group_heads, devices, portion), 'seq',...  16.4 us
    all_gather x1, waiting for transfers between devices, per_device(): full_grad = lax.all_gather(out_cotangent, 'head', axis=1, tiled=True)  16.3 us
    all_to_all x1, starting transfers between devices, per_device(): lax.all_to_all(stacked.reshape(2, group_heads, devices, portion), 'seq',...  13 us
    all_to_all x1, starting transfers between devices, per_device(): lax.all_to_all(picked, 'seq', split_axis=3, concat_axis=3, tiled=True)  9.32 us
    all_to_all x1, starting transfers between devices, per_device(): lax.all_to_all(summed_back, 'seq', split_axis=2, concat_axis=2, tiled=True)  8.6 us
  transfers between devices with their start and end apart: 7, of which 5 were waited for; matrix products, arithmetic and copies ran while one was open for 8% of the time, Pallas kernels for 0%

commit v1 on v0

--- a/solution.py
+++ b/solution.py
@@ -63,7 +63,10 @@
     columns = summed.shape[1] // lax.axis_size("head")
     result = lax.dynamic_slice_in_dim(summed, lax.axis_index("head") * columns, columns, 1)
     projected = result.astype(jnp.bfloat16)
-    full_grad = lax.all_gather(out_cotangent, "head", axis=1, tiled=True)
+    peers = lax.axis_size("head")
+    blocks = jnp.stack([out_cotangent for _ in range(peers)])
+    blocks = lax.all_to_all(blocks, "head", split_axis=0, concat_axis=0)
+    full_grad = jnp.concatenate(blocks, axis=1)
     grad_att = jnp.einsum(
         "te,hde->htd", full_grad, out_weight, preferred_element_type=jnp.float32
     ).astype(jnp.bfloat16)

time: 316 us -> 347 us (1.098)
  blocking collectives: 45.1 us -> 65.4 us
  local copies, waits for them, and re-layouts: 23.7 us -> 30 us
    all_to_all x0 -> x1, blocking collectives: none -> 29.5 us  [per_device(): lax.all_to_all(stacked.reshape(2, group_heads, devices, portion), 'seq',...]
    all_to_all x1, waiting for transfers between devices: 16.4 us -> 43.8 us  [per_device(): blocks = lax.all_to_all(blocks, 'head', split_axis=0, concat_axis=0)]
    all_gather x1 -> x0, waiting for transfers between devices: 16.3 us -> none  [per_device(): full_grad = lax.all_gather(out_cotangent, 'head', axis=1, tiled=True)]
    all_to_all x1, blocking collectives: 45.1 us -> 35.9 us  [per_device(): lax.all_to_all(partner_grad.reshape(2, group_heads, slot_count, devices,...]
    all_to_all x1, waiting for transfers between devices: 21.5 us -> 15.2 us  [per_device(): lax.all_to_all(picked, 'seq', split_axis=3, concat_axis=3, tiled=True)]
    psum x1, waiting for transfers between devices: 111 us -> 106 us  [per_device(): lax.psum(partial_out.astype(jnp.bfloat16), 'head').astype(jnp.float32)]
    reshape x0 -> x2, local copies, waits for them, and re-layouts: none -> 4.37 us  [per_device(): full_grad = jnp.concatenate(blocks, axis=1)]
    all_to_all x1, starting transfers between devices: 9.32 us -> 12.9 us  [per_device(): lax.all_to_all(picked, 'seq', split_axis=3, concat_axis=3, tiled=True)]
  transfers between devices with their start and end apart: 7 -> 6, of which waited for: 5 -> 4; matrix products, arithmetic and copies ran while one was open for 8% -> 7% of each run, Pallas kernels for 0% -> 0%
where the time goes in v1:
time: 347 us; the launch traced here: 346 us
  waiting for transfers between devices  167 us (48%)
  blocking collectives  65.4 us (19%)
  starting transfers between devices  38.3 us (11%)
  local copies, waits for them, and re-layouts  30 us (9%)
  other arithmetic  15.8 us (5%)
  matrix products  15 us (4%)
  between operations  14.4 us (4%)
    psum x1, waiting for transfers between devices, per_device(): lax.psum(partial_out.astype(jnp.bfloat16), 'head').astype(jnp.float32)  106 us
    all_to_all x1, waiting for transfers between devices, per_device(): blocks = lax.all_to_all(blocks, 'head', split_axis=0, concat_axis=0)  43.8 us
    all_to_all x1, blocking collectives, per_device(): lax.all_to_all(partner_grad.reshape(2, group_heads, slot_count, devices,...  35.9 us
    all_to_all x1, blocking collectives, per_device(): lax.all_to_all(stacked.reshape(2, group_heads, devices, portion), 'seq',...  29.5 us
    all_to_all x1, waiting for transfers between devices, per_device(): lax.all_to_all(picked, 'seq', split_axis=3, concat_axis=3, tiled=True)  15.2 us
    all_to_all x1, starting transfers between devices, per_device(): lax.all_to_all(picked, 'seq', split_axis=3, concat_axis=3, tiled=True)  12.9 us
    all_to_all x1, starting transfers between devices, per_device(): blocks = lax.all_to_all(blocks, 'head', split_axis=0, concat_axis=0)  12.4 us
    all_to_all x1, starting transfers between devices, per_device(): lax.all_to_all(summed_back, 'seq', split_axis=2, concat_axis=2, tiled=True)  8.72 us
  transfers between devices with their start and end apart: 6, of which 4 were waited for; matrix products, arithmetic and copies ran while one was open for 7% of the time, Pallas kernels for 0%

profile of v1, /device:TPU:2, one launch (start us, length us, event | category | flops | bytes accessed | tf_op | source)
XLA Modules:
  0.0 346.3 jit_solution(5306199015065881151)
XLA Ops:
  10.1 29.5 %all_to_all.25 = bf16[2,4,128,256]{3,0,1,2:T(2,128)(2,1)} all-to-all(bf16[2,4,128,256]{3,0,1,2:T(2,128)(2,1)S(1)} %copy.74), channel_id=1, replica_groups=mesh['seq'=128,'head'=4] {'seq'}, dimensions={2} | all-to-all | bytes 1048576 | tf_op jit(solution)/shard_map/all_to_all | solution.py:26
  40.6 12.4 %all-to-all-start.2 = ((bf16[4,256,512]{2,1,0:T(8,128)(2,1)}), bf16[4,256,512]{2,1,0:T(8,128)(2,1)S(1)}, u32[]{:S(2)}, u32[]{:S(2)}) async-start(bf16[4,256,512]{2,1,0:T(8,128)(2,1)} %stack.43), calls=%async_computation.2 | async-start | bytes 2097152 | tf_op jit(solution)/shard_map/all_to_all | solution.py:68
  53.2 2.7 fusion.11
  55.9 3.7 %copy.78 = bf16[2,4,2,128,256]{4,2,0,1,3:T(2,128)(2,1)} copy(bf16[2,4,2,128,256]{3,4,2,0,1:T(8,128)(2,1)} %fusion.11) | data formatting | bytes 2097152 | tf_op jit(solution)/shard_map/convert_element_type | solution.py:35
  59.6 43.8 %all-to-all-done.2 = bf16[4,256,512]{2,1,0:T(8,128)(2,1)S(1)} async-done(((bf16[4,256,512]{2,1,0:T(8,128)(2,1)}), bf16[4,256,512]{2,1,0:T(8,128)(2,1)S(1)}, u32[]{:S(2)}, u32[]{:S(2)}) %all-to-all-start.2) | async-done | bytes 1048608 | tf_op jit(solution)/shard_map/all_to_all | solution.py:68
  103.4 12.9 %all-to-all-start.1 = ((bf16[2,4,2,128,256]{4,2,0,1,3:T(2,128)(2,1)}), bf16[2,4,2,128,256]{4,2,0,1,3:T(2,128)(2,1)}, u32[]{:S(2)}, u32[]{:S(2)}) async-start(bf16[2,4,2,128,256]{4,2,0,1,3:T(2,128)(2,1)} %copy.78), calls=%async_computation.1 | async-start | bytes 2097152 | tf_op jit(solution)/shard_map/all_to_all | solution.py:36
  116.3 1.8 pad_maximum_fusion.2
  118.1 2.2 collective-permute-start
  120.4 1.9 collective-permute-done
  122.3 1.7 maximum_select_fusion
  124.0 1.8 copy.83
  125.8 2.6 reshape.69
  128.4 15.2 %all-to-all-done.1 = bf16[2,4,2,128,256]{4,2,0,1,3:T(2,128)(2,1)} async-done(((bf16[2,4,2,128,256]{4,2,0,1,3:T(2,128)(2,1)}), bf16[2,4,2,128,256]{4,2,0,1,3:T(2,128)(2,1)}, u32[]{:S(2)}, u32[]{:S(2)}) %all-to-all-start.1) | async-done | bytes 1048608 | tf_op jit(solution)/shard_map/all_to_all | solution.py:36
  143.5 2.5 copy.79
  146.1 2.3 reshape_reshape.3
  148.4 2.1 fusion.15
  150.4 4.6 %fusion.35 = (f32[4,256]{1,0:T(4,128)S(1)}, f32[4,256,1024]{1,2,0:T(8,128)}) fusion(bf16[4,1024,128]{2,1,0:T(8,128)(2,1)} %fusion.15, bf16[4,256,128]{2,1,0:T(8,128)(2,1)S(1)} %copy-done.14), kind=kOutput, calls=%fused_computation.62 | convolution fusion | flops 271582208 | bytes 5509120 | tf_op jit(solution)/shard_map/sub | solution.py:53
  155.1 2.6 fusion.10
  160.4 2.2 copy-done.8
  164.9 1.3 copy-done.2
  167.7 2.3 copy.89
  170.0 35.9 %all_to_all.26 = bf16[2,4,2,128,256]{4,2,0,1,3:T(2,128)(2,1)S(1)} all-to-all(bf16[2,4,2,128,256]{4,2,0,1,3:T(2,128)(2,1)S(1)} %copy.89), channel_id=1, replica_groups=mesh['seq'=128,'head'=4] {'seq'}, dimensions={3} | all-to-all | bytes 2097152 | tf_op jit(solution)/shard_map/all_to_all | solution.py:100
  207.8 8.7 %all-to-all-start.4 = ((bf16[2,4,128,256]{3,0,1,2:T(2,128)(2,1)}), bf16[2,4,128,256]{3,0,1,2:T(2,128)(2,1)S(1)}, u32[]{:S(2)}, u32[]{:S(2)}) async-start(bf16[2,4,128,256]{3,0,1,2:T(2,128)(2,1)} %copy.91), calls=%async_computation.4 | async-start | bytes 1048576 | tf_op jit(solution)/shard_map/all_to_all | solution.py:110
  216.6 1.8 fusion.6
  218.5 1.8 fusion.7
  220.3 1.3 copy-done.3
  222.5 2.0 collective-permute-start.1
  224.6 1.6 convolution_convert_fusion.1
  226.2 106.4 %all-reduce.2.cloned.1.call-done = bf16[256,2048]{1,0:T(8,128)(2,1)} async-done(((bf16[256,2048]{1,0:T(8,128)(2,1)}), bf16[256,2048]{1,0:T(8,128)(2,1)}) %all-reduce.2.cloned.1.call-update) | async-done | bytes 1048592 | tf_op jit(solution)/shard_map/psum | solution.py:62
  332.6 1.7 convert_convert_fusion
  335.4 1.3 reshape.65
  336.7 1.9 fusion.18
  (58 shorter events, 15.4 us)
Async XLA Ops:
  7.2 151.1 %copy-start = (bf16[4,128,2048]{2,1,0:T(8,128)(2,1)S(1)}, bf16[4,128,2048]{2,1,0:T(8,128)(2,1)}, u32[]{:S(2)}) copy-start(bf16[4,128,2048]{2,1,0:T(8,128)(2,1)} %param.10) | copy-start | bytes 6291460
  7.2 32.4 %copy-start.13 = (bf16[256,512]{1,0:T(8,128)(2,1)S(1)}, bf16[256,512]{1,0:T(8,128)(2,1)}, u32[]{:S(2)}) copy-start(bf16[256,512]{1,0:T(8,128)(2,1)} %param.11) | copy-start | bytes 786436
  10.0 43.0 %copy-start.16 = (s32[4,64]{1,0:T(4,128)S(1)}, s32[4,64]{1,0:T(4,128)}, u32[]{:S(2)}) copy-start(s32[4,64]{1,0:T(4,128)} %param.9) | copy-start | bytes 3076
  40.6 62.8 %all-to-all-start.2 = ((bf16[4,256,512]{2,1,0:T(8,128)(2,1)}), bf16[4,256,512]{2,1,0:T(8,128)(2,1)S(1)}, u32[]{:S(2)}, u32[]{:S(2)}) async-start(bf16[4,256,512]{2,1,0:T(8,128)(2,1)} %stack.43), calls=%async_computation.2 | async-start | bytes 2097152 | tf_op jit(solution)/shard_map/all_to_all | solution.py:68
  55.9 60.4 %copy-start.11 = (bf16[4,256,128]{2,1,0:T(8,128)(2,1)S(1)}, bf16[4,256,128]{2,1,0:T(8,128)(2,1)}, u32[]{:S(2)}) copy-start(bf16[4,256,128]{2,1,0:T(8,128)(2,1)} %param.8) | copy-start | bytes 786436
  103.4 17.0 %copy-start.9 = (bf16[4,256,512]{2,1,0:T(8,128)(2,1)}, bf16[4,256,512]{2,1,0:T(8,128)(2,1)S(1)}, u32[]{:S(2)}) copy-start(bf16[4,256,512]{2,1,0:T(8,128)(2,1)S(1)} %all-to-all-done.2) | copy-start | bytes 3145732
  103.4 40.1 %all-to-all-start.1 = ((bf16[2,4,2,128,256]{4,2,0,1,3:T(2,128)(2,1)}), bf16[2,4,2,128,256]{4,2,0,1,3:T(2,128)(2,1)}, u32[]{:S(2)}, u32[]{:S(2)}) async-start(bf16[2,4,2,128,256]{4,2,0,1,3:T(2,128)(2,1)} %copy.78), calls=%async_computation.1 | async-start | bytes 2097152 | tf_op jit(solution)/shard_map/all_to_all | solution.py:36
  118.1 4.1 %collective-permute-start = (bf16[2,4,256,128]{3,2,1,0:T(8,128)(2,1)}, bf16[2,4,256,128]{3,2,1,0:T(8,128)(2,1)}, u32[]{:S(2)}, u32[]{:S(2)}) collective-permute-start(bf16[2,4,256,128]{3,2,1,0:T(8,128)(2,1)} %pad_maximum_fusion.2), channel_id=1, source_target_pairs={{0,4},{4,0},{8,12},{12,8},{16,20},{20,16},{24,28},{28,24},{32,36},... | collective-permute-start | bytes 1572872 | tf_op jit(solution)/shard_map/ppermute | solution.py:9
  122.3 1.7 copy-start.10
  146.1 4.4 %copy-start.14 = (bf16[4,256,128]{2,1,0:T(8,128)(2,1)S(1)}, bf16[4,256,128]{2,1,0:T(8,128)(2,1)}, u32[]{:S(2)}) copy-start(bf16[4,256,128]{2,1,0:T(8,128)(2,1)} %param.6) | copy-start | bytes 786436
  155.1 2.6 copy-start.4
  157.7 1.2 copy-start.12
  159.7 2.9 copy-start.8
  160.4 3.9 %copy-start.1 = (f32[1,4,1024,128]{3,2,1,0:T(8,128)}, f32[1,4,1024,128]{3,2,1,0:T(8,128)S(1)}, u32[]{:S(2)}) copy-start(f32[1,4,1024,128]{3,2,1,0:T(8,128)S(1)} %convolution_bitcast_fusion.1) | copy-start | bytes 6291460
  162.6 0.9 copy-start.15
  163.6 1.3 copy-start.5
  164.9 1.3 copy-start.2
  207.8 126.4 %all-to-all-start.4 = ((bf16[2,4,128,256]{3,0,1,2:T(2,128)(2,1)}), bf16[2,4,128,256]{3,0,1,2:T(2,128)(2,1)S(1)}, u32[]{:S(2)}, u32[]{:S(2)}) async-start(bf16[2,4,128,256]{3,0,1,2:T(2,128)(2,1)} %copy.91), calls=%async_computation.4 | async-start | bytes 1048576 | tf_op jit(solution)/shard_map/all_to_all | solution.py:110
  216.6 116.0 %all-reduce.2.cloned.1.call-start = ((), (), s32[]{:S(2)}) async-start(), calls=%async_computation.5 | async-start | bytes 2097152 | tf_op jit(solution)/shard_map/psum | solution.py:62
  218.4 6.1 %copy-start.6 = (bf16[4,256,1024]{1,2,0:T(8,128)(2,1)S(1)}, bf16[4,256,1024]{1,2,0:T(8,128)(2,1)}, u32[]{:S(2)}) copy-start(bf16[4,256,1024]{1,2,0:T(8,128)(2,1)} %copy-done.5) | copy-start | bytes 6291460
  218.4 6.1 %copy-start.7 = (bf16[4,1024,128]{2,1,0:T(8,128)(2,1)S(1)}, bf16[4,1024,128]{2,1,0:T(8,128)(2,1)}, u32[]{:S(2)}) copy-start(bf16[4,1024,128]{2,1,0:T(8,128)(2,1)} %fusion.15) | copy-start | bytes 3145732
  220.3 1.3 copy-start.3
  222.5 114.1 %collective-permute-start.1 = (bf16[2,4,256,128]{3,2,1,0:T(8,128)(2,1)}, bf16[2,4,256,128]{3,2,1,0:T(8,128)(2,1)}, u32[]{:S(2)}, u32[]{:S(2)}) collective-permute-start(bf16[2,4,256,128]{3,2,1,0:T(8,128)(2,1)} %fusion.20), channel_id=1, source_target_pairs={{0,4},{4,0},{8,12},{12,8},{16,20},{20,16},{24,28},{28,24},{32,36},... | collective-permute-start | bytes 1572872 | tf_op jit(solution)/shard_map/ppermute | solution.py:9
Sparse Core Ops, SparseCore 0:
  220.4 112.2 all-reduce.1
